TPU v7x, 256 devices: a whole 4x4x8 slice. The times are simulated.
256 devices in a mesh: hier: 16 (over x_hi, z), row: 16 (over x_lo, y, core).
Axes of the slice: x: 4 (x_hi: 2, x_lo: 2; x = x_hi * 2 + x_lo), y: 4, z: 8, core: 2. Of those that a mesh axis runs over, the one named last changes fastest.
Arguments:
- state: bfloat16 [48, 2, 1024, 1024], P('hier', None, 'row'), may hold values from -6 to 6
- prev_slope: float32 [48, 2, 1024, 1024], P('hier', None, 'row'), may hold values from -6 to 6
- accumulated: float32 [48, 2, 1024, 1024], P('hier', None, 'row'), may hold values from -6 to 6
- hamiltonian: bfloat16 [2, 1024, 1024], P(None, 'row'), as said below
- couple_v: float32 [6, 1024], replicated, may hold values from -4 to 4
- coupling: float32 [2, 6], replicated, may hold values from 0.2 to 1
- damping: float32 [6], replicated, may hold values from 0.2 to 2
- occupation: int32 [48, 6], P('hier'), may hold values from 0 to 3, as said below
- parents: int32 [48, 6], P('hier'), may hold values from -1 to 47, as said below
- children: int32 [48, 6], P('hier'), may hold values from -1 to 46, as said below
Outputs:
- slope: float32 [48, 2, 1024, 1024], P('hier', None, 'row')
- accumulated_out: float32 [48, 2, 1024, 1024], P('hier', None, 'row')
Inputs may be any that keep to these rules, and one draw needn't show every extreme that they name: `occupation`: row s is the index of the operator in slot s. The rows are the 48 indices of smallest total among all indices of 6 entries with total at most 4, taken by total and then lexicographically; the all-zero index stands in the last slot, the others in a slot order drawn from the seed; the set is closed under lowering one entry. `parents`: entry (s, k) is the slot whose index equals slot s's index with entry k lowered by one, or -1 where entry k of slot s is 0. `children`: entry (s, k) is the slot whose index equals slot s's index with entry k raised by one, or -1 where that index is not among the 48. `hamiltonian`: Hermitian: the real part is symmetric, the imaginary part antisymmetric.
All inputs are finite; a program needn't handle non-finite values.
Results may differ from a plain program's by a relative error of at most 0.0029.
Values may be sent and summed in bfloat16 or wider, within the bound.
A program may use at most 192 MiB of HBM per device.

v0:
```python
import jax
import jax.numpy as jnp
import numpy as np
from jax import lax
from jax.experimental import pallas as pl
from jax.experimental.pallas import tpu as pltpu
from jax.sharding import PartitionSpec as P

MESH = pl.DeviceIdType.MESH
N = 1024
MODES = 6
ADOS = 48
STEP = 0.5
F32 = jnp.float32
BF16 = jnp.bfloat16


def window_table():
    entries = [()]
    for _ in range(MODES):
        entries = [entry + (level,) for entry in entries for level in range(5)]
    chosen = [entry for entry in entries if sum(entry) <= 4]
    return sorted(chosen, key=lambda entry: (sum(entry), entry))[:ADOS]


TABLE = window_table()
PLACE = {entry: place for place, entry in enumerate(TABLE)}


def key_of(entry):
    return sum(entry[k] * 5**k for k in range(MODES))


def shifted(entry, mode, by):
    return PLACE.get(entry[:mode] + (entry[mode] + by,) + entry[mode + 1 :])


def key_table():
    keys = np.full((8, 128), -1, np.int32)
    keys[:, :ADOS] = [key_of(entry) for entry in TABLE]
    return keys


R_HN = 0
R_HU = 1
R_HD = 3
R_H2 = 5
R_HP = 7
R_L = 15
R_LP = 23
R_LR = 31
R_XR = 39
R_X = 41
R_Z = 43
R_ZX = 51
R_M = 59
R_C = 75
R_CX = 83
R_CR = 91
R_CF = 93
N_RECV = 95
N_SEND = 110


def kernel(
    state,
    prev,
    ham,
    cv,
    coup,
    damp,
    occ,
    tab,
    slope,
    st_v,
    pv_v,
    sblk,
    amat,
    hn,
    lb,
    lout,
    lret,
    zin,
    xin,
    xrp,
    xrm,
    ccan,
    cout,
    cx,
    crp,
    crm,
    cret,
    rbuf,
    meta_out,
    meta_in,
    meta_v,
    meta_s,
    vt,
    dk,
    dg,
    eg,
    lsem,
    ssem,
    rsem,
):
    h = lax.axis_index("hier")
    r = lax.axis_index("row")
    xh, z = lax.div(h, 8), lax.rem(h, 8)
    p, c = lax.div(r, 2), lax.rem(r, 2)
    xl, y = lax.div(p, 4), lax.rem(p, 4)
    oc = 1 - c

    def chip(dx, dy):
        return lax.rem(xl + dx, 2) * 4 + lax.rem(y + dy, 4)

    def zrow(dz):
        return lax.rem(z + dz, 8)

    def rowdev(dx, dy):
        return (h, chip(dx, dy) * 2 + c)

    def zdev(dz):
        return (xh * 8 + zrow(dz), r)

    other_core = (h, p * 2 + oc)
    other_row = ((1 - xl) * 4 + y) * 2 + c
    xhp = lax.rem(xh + xl, 2)
    xhm = lax.rem(xh + 1 - xl, 2)
    x_up = (xhp * 8 + z, other_row)
    x_down = (xhm * 8 + z, other_row)
    x_cross = ((1 - xh) * 8 + z, other_row)
    h2 = (1 - xh) * 8 + z

    row_offsets = [(dx, dy) for dy in (1, 3, 0, 2) for dx in (0, 1) if dx or dy]
    z_offsets = [4, 3, 5, 2, 6, 1, 7]

    cp_h = pltpu.make_async_copy(ham, hn.at[:, p, c], lsem.at[0])
    cp_s = pltpu.make_async_copy(state, st_v, lsem.at[1])
    cp_p = pltpu.make_async_copy(prev, pv_v, lsem.at[2])
    cp_h.start()
    cp_s.start()
    cp_p.start()

    barrier = pltpu.get_barrier_semaphore()
    greeted = [rowdev(dx, dy) for dx, dy in row_offsets]
    greeted += [other_core, x_cross]
    greeted += [(lax.rem(h + d, 16), r) for d in range(1, 16)]
    for dev in greeted:
        pl.semaphore_signal(barrier, inc=1, device_id=dev, device_id_type=MESH)

    lane = lax.broadcasted_iota(jnp.int32, (8, 128), 1)
    line = lax.broadcasted_iota(jnp.int32, (8, 128), 0)
    slots = jnp.zeros((8, 128), jnp.int32)
    places = jnp.zeros((8, 128), jnp.int32)
    for j in range(3):
        key = occ[j, 0]
        for k in range(1, MODES):
            key = key + occ[j, k] * (5**k)
        hit = tab[...] == key
        slots = slots + jnp.where(hit, 3 * h + j, 0)
        place = jnp.sum(jnp.where(hit, lane, 0), axis=1, keepdims=True)
        places = places + jnp.where(lane == 3 * h + j, place, 0)
    mine = jnp.where(line == 0, slots, places)
    meta_out[...] = mine

    pl.semaphore_wait(barrier, len(greeted))

    sent = []

    def send(src, dst, to, dev):
        copy = pltpu.make_async_remote_copy(
            src_ref=src,
            dst_ref=dst,
            send_sem=ssem.at[len(sent)],
            recv_sem=rsem.at[to],
            device_id=dev,
            device_id_type=MESH,
        )
        copy.start()
        sent.append(copy)

    def arrived(dst, to):
        pltpu.make_async_remote_copy(
            src_ref=dst,
            dst_ref=dst,
            send_sem=ssem.at[0],
            recv_sem=rsem.at[to],
            device_id=other_core,
            device_id_type=MESH,
        ).wait_recv()

    def hblk(q):
        return hn.at[:, q, c]

    def send_h(q, to, dev):
        send(hblk(q), hblk(q), to, dev)

    cp_h.wait()
    send_h(p, R_HN, x_cross)
    send_h(p, R_HU, rowdev(0, 1))
    send_h(p, R_HD, rowdev(0, 3))
    send_h(p, R_HP, other_core)

    cp_s.wait()
    cp_p.wait()

    @pl.loop(0, 3)
    def _(a):
        for half in range(2):
            rows = pl.ds(32 * half, 32)
            for b in range(8):
                cols = pl.ds(128 * b, 128)
                parts = []
                for ri in range(2):
                    value = st_v[a, ri, rows, cols].astype(F32) + (0.5 * STEP) * pv_v[a, ri, rows, cols]
                    parts.append(value.astype(BF16))
                    sblk[b, half, a, ri] = parts[ri]
                    amat[half, a, ri, :, cols] = parts[ri]
                late = pl.ds(N + 128 * b, 128)
                amat[half, a, 0, :, late] = -parts[1]
                amat[half, a, 1, :, late] = parts[0]

    send(sblk.at[pl.ds(0, 4), 1 - xh], xrp, R_XR, x_up)
    send(sblk.at[pl.ds(4, 4), 1 - xh], xrm, R_XR + 1, x_down)
    for dz in z_offsets:
        send(sblk.at[zrow(dz), xh], zin.at[pl.ds(3 * h, 3)], R_Z + dz, zdev(dz))
    for dx, dy in row_offsets:
        q = chip(dx, dy)
        send(sblk.at[q], lb.at[p, c], R_L + 4 * dx + dy, (h, q * 2 + c))
    send(sblk.at[p], lb.at[p, c], R_LP, other_core)
    for d in range(1, 16):
        send(meta_out, meta_in.at[h], R_M + d, (lax.rem(h + d, 16), r))
    meta_in[h] = mine
    lb[p, c] = sblk[p]
    zin[pl.ds(3 * h, 3)] = sblk[z, xh]

    arrived(xrp, R_XR)
    send(xrp, xin.at[pl.ds(0, 4)], R_X, x_up)
    arrived(xrm, R_XR + 1)
    send(xrm, xin.at[pl.ds(4, 4)], R_X + 1, x_down)

    q = chip(1, 0)
    arrived(hblk(q), R_HN)
    send_h(q, R_HU + 1, rowdev(0, 1))
    send_h(q, R_HD + 1, rowdev(0, 3))
    send_h(q, R_HP + 4, other_core)

    for k in range(MODES):
        line_v = cv[pl.ds(k, 1), pl.ds(pl.multiple_of(128 * p, 128), 128)]
        vt[k] = jnp.broadcast_to(line_v, (128, 128)).T
        v_rows = vt[k, pl.ds(pl.multiple_of(64 * c + 32 * xh, 32), 32), :]
        v_cols = cv[pl.ds(k, 1), pl.ds(pl.multiple_of(128 * z, 128), 128)]
        diff = v_rows - v_cols
        dk[k] = diff
        dg[k] = coup[0, k] * diff
        eg[k] = coup[1, k] * (v_rows + v_cols)

    arrived(xin.at[pl.ds(0, 4)], R_X)
    arrived(xin.at[pl.ds(4, 4)], R_X + 1)
    for dz in z_offsets:
        send(xin.at[zrow(dz)], zin.at[pl.ds(3 * h2, 3)], R_ZX + dz, zdev(dz))
    zin[pl.ds(3 * h2, 3)] = xin[z]

    for dx, dy in row_offsets:
        back = (4 - dy) % 4
        q = chip(dx, back)
        arrived(lb.at[q, c], R_L + 4 * dx + dy)
        send(lb.at[q, c], lb.at[q, c], R_LP + 4 * dx + back, other_core)

    for dx in range(2):
        arrived(hblk(chip(dx, 3)), R_HU + dx)
        send_h(chip(dx, 3), R_HP + 4 * dx + 3, other_core)
        arrived(hblk(chip(dx, 1)), R_HD + dx)
        send_h(chip(dx, 1), R_HP + 4 * dx + 1, other_core)
    send_h(lax.rem(y + 3, 4), R_H2, rowdev(0, 1))
    send_h(4 + lax.rem(y + 1, 4), R_H2 + 1, rowdev(0, 3))

    for d in range(1, 16):
        arrived(meta_in.at[lax.rem(h + 16 - d, 16)], R_M + d)
    meta_v[...] = jnp.minimum(jnp.sum(meta_in[...], axis=0), ADOS - 1)
    cp_m = pltpu.make_async_copy(meta_v, meta_s, lsem.at[3])
    cp_m.start()
    for dz in z_offsets:
        zs = zrow(8 - dz)
        arrived(zin.at[pl.ds(3 * (xh * 8 + zs), 3)], R_Z + dz)
        arrived(zin.at[pl.ds(3 * ((1 - xh) * 8 + zs), 3)], R_ZX + dz)
    cp_m.wait()
    for place, entry in enumerate(TABLE):
        re = jnp.zeros((32, 128), F32)
        im = jnp.zeros((32, 128), F32)
        for k in range(MODES):
            child = shifted(entry, k, 1)
            if child is not None:
                near = zin[meta_s[0, child]].astype(F32)
                re = re + dk[k] * near[1]
                im = im - dk[k] * near[0]
            if entry[k] > 0:
                near = zin[meta_s[0, shifted(entry, k, -1)]].astype(F32)
                add_re = dg[k] * near[1] + eg[k] * near[0]
                add_im = eg[k] * near[1] - dg[k] * near[0]
                if entry[k] > 1:
                    add_re = add_re * float(entry[k])
                    add_im = add_im * float(entry[k])
                re = re + add_re
                im = im + add_im
        ccan[place, 0] = re.astype(BF16)
        ccan[place, 1] = im.astype(BF16)
    for slot in range(ADOS):
        cout[slot] = ccan[meta_s[1, slot]]
    for dz in z_offsets:
        send(cout.at[pl.ds(3 * ((1 - xh) * 8 + zrow(dz)), 3)], cx.at[z], R_CX + dz, zdev(dz))
    for dz in z_offsets:
        send(cout.at[pl.ds(3 * (xh * 8 + zrow(dz)), 3)], cret.at[xh, z], R_C + dz, zdev(dz))
    cx[z] = cout[pl.ds(3 * h2, 3)]
    cret[xh, z] = cout[pl.ds(3 * h, 3)]

    arrived(hblk(lax.rem(y + 2, 4)), R_H2)
    send_h(lax.rem(y + 2, 4), R_HP + 2, other_core)
    arrived(hblk(4 + lax.rem(y + 2, 4)), R_H2 + 1)
    send_h(4 + lax.rem(y + 2, 4), R_HP + 6, other_core)
    for dx in range(2):
        for dy in range(4):
            arrived(lb.at[chip(dx, dy), oc], R_LP + 4 * dx + dy)

    @pl.loop(0, 3)
    def _(a):
        real = lb[:, :, :, a, 0].reshape(N, 128)
        imag = lb[:, :, :, a, 1].reshape(N, 128)
        rhs = jnp.concatenate(
            [jnp.concatenate([real, imag], 1), jnp.concatenate([-imag, real], 1)], 0
        )
        for m in range(2):
            lhs = jnp.concatenate(
                [hn[ri, pl.ds(4 * m, 4), c].reshape(256, N) for ri in range(2)], 1
            )
            out = jnp.dot(lhs, rhs, preferred_element_type=F32).astype(BF16)
            out = out.reshape(4, 2, 32, 256)
            lout[pl.ds(4 * m, 4), :, a, 0] = out[..., :128]
            lout[pl.ds(4 * m, 4), :, a, 1] = out[..., 128:]

    for dx, dy in row_offsets:
        q = chip(dx, dy)
        send(lout.at[q], lret.at[p], R_LR + 4 * dx + dy, (h, q * 2 + c))
    lret[p] = lout[p]

    for dx in range(2):
        for dy in range(4):
            if dy == 2:
                q = 4 * dx + lax.rem(y + 2, 4)
            else:
                q = chip(dx, dy)
            arrived(hn.at[:, q, oc], R_HP + 4 * dx + dy)

    @pl.loop(0, 4)
    def _(n):
        cols = pl.ds(pl.multiple_of(256 * n, 256), 256)
        rhs = jnp.concatenate(
            [hn[ri, :, :, :, cols].reshape(N, 256) for ri in range(2)], 0
        )
        lhs = amat[...].reshape(384, 2 * N)
        out = jnp.dot(lhs, rhs, preferred_element_type=F32)
        rbuf[:, :, :, :, cols] = out.reshape(2, 3, 2, 32, 256)

    for dz in z_offsets:
        arrived(cx.at[zrow(8 - dz)], R_CX + dz)
    send(cx.at[pl.ds(0, 4)], crp, R_CR, x_up)
    send(cx.at[pl.ds(4, 4)], crm, R_CR + 1, x_down)
    arrived(crp, R_CR)
    send(crp, cret.at[1 - xhp, pl.ds(0, 4)], R_CF, x_up)
    arrived(crm, R_CR + 1)
    send(crm, cret.at[1 - xhm, pl.ds(4, 4)], R_CF + 1, x_down)

    for dx, dy in row_offsets:
        back = (4 - dy) % 4
        arrived(lret.at[chip(dx, back)], R_LR + 4 * dx + dy)
    for dz in z_offsets:
        arrived(cret.at[xh, zrow(8 - dz)], R_C + dz)
    arrived(cret.at[1 - xh, pl.ds(0, 4)], R_CF)
    arrived(cret.at[1 - xh, pl.ds(4, 4)], R_CF + 1)

    @pl.loop(0, 3)
    def _(a):
        decay = occ[a, 0].astype(F32) * damp[0]
        for k in range(1, MODES):
            decay = decay + occ[a, k].astype(F32) * damp[k]
        for half in range(2):
            for b in range(8):
                cols = pl.ds(128 * b, 128)
                for ri in range(2):
                    turned = lret[b, half, a, 1 - ri].astype(F32) - rbuf[half, a, 1 - ri, :, cols]
                    if ri:
                        turned = -turned
                    value = turned - decay * sblk[b, half, a, ri].astype(F32)
                    value = value + cret[half, b, a, ri].astype(F32)
                    slope[a, ri, pl.ds(32 * half, 32), cols] = value

    for copy in sent:
        copy.wait_send()


def shards(state, prev_slope, accumulated, hamiltonian, couple_v, coupling, damping, occupation, parents, children):
    vmem = pltpu.VMEM
    anywhere = pl.BlockSpec(memory_space=pl.ANY)
    in_vmem = pl.BlockSpec(memory_space=pltpu.VMEM)
    in_smem = pl.BlockSpec(memory_space=pltpu.SMEM)
    slope = pl.pallas_call(
        kernel,
        name="section",
        out_shape=jax.ShapeDtypeStruct((3, 2, 64, N), F32),
        in_specs=[anywhere, anywhere, anywhere, in_vmem, in_smem, in_smem, in_smem, in_vmem],
        out_specs=in_vmem,
        scratch_shapes=[
            vmem((3, 2, 64, N), BF16),
            vmem((3, 2, 64, N), F32),
            vmem((8, 2, 3, 2, 32, 128), BF16),
            vmem((2, 3, 2, 32, 2 * N), BF16),
            vmem((2, 8, 2, 64, N), BF16),
            vmem((8, 2, 2, 3, 2, 32, 128), BF16),
            vmem((8, 2, 3, 2, 32, 128), BF16),
            vmem((8, 2, 3, 2, 32, 128), BF16),
            vmem((ADOS, 2, 32, 128), BF16),
            vmem((8, 3, 2, 32, 128), BF16),
            vmem((4, 3, 2, 32, 128), BF16),
            vmem((4, 3, 2, 32, 128), BF16),
            vmem((ADOS, 2, 32, 128), BF16),
            vmem((ADOS, 2, 32, 128), BF16),
            vmem((8, 3, 2, 32, 128), BF16),
            vmem((4, 3, 2, 32, 128), BF16),
            vmem((4, 3, 2, 32, 128), BF16),
            vmem((2, 8, 3, 2, 32, 128), BF16),
            vmem((2, 3, 2, 32, N), F32),
            vmem((8, 128), jnp.int32),
            vmem((16, 8, 128), jnp.int32),
            vmem((8, 128), jnp.int32),
            pltpu.SMEM((8, 128), jnp.int32),
            vmem((MODES, 128, 128), F32),
            vmem((MODES, 32, 128), F32),
            vmem((MODES, 32, 128), F32),
            vmem((MODES, 32, 128), F32),
            pltpu.SemaphoreType.DMA((4,)),
            pltpu.SemaphoreType.DMA((N_SEND,)),
            pltpu.SemaphoreType.DMA((N_RECV,)),
        ],
        compiler_params=pltpu.CompilerParams(collective_id=0, has_side_effects=True),
    )(state, prev_slope, hamiltonian, couple_v, coupling, damping, occupation, jnp.asarray(key_table()))
    return slope, accumulated + (STEP / 3.0) * slope


def solution(mesh):
    block = P("hier", None, "row", None)
    return jax.shard_map(
        shards,
        mesh=mesh,
        in_specs=(
            block,
            block,
            block,
            P(None, "row", None),
            P(),
            P(),
            P(),
            P("hier", None),
            P("hier", None),
            P("hier", None),
        ),
        out_specs=(block, block),
        check_vma=False,
    )
```

profile of v0, /device:TPU:24, one launch (start us, length us, event | category | flops | bytes accessed | tf_op | source)
XLA Modules:
  0.0 71.2 jit_solution(16972588774593680287)
XLA Ops:
  0.6 0.0 copy-start.1
  0.6 66.4 %section.1 = f32[3,2,64,1024]{3,2,1,0:T(8,128)} custom-call(bf16[3,2,64,1024]{3,2,1,0:T(8,128)(2,1)} %state.1, f32[3,2,64,1024]{3,2,1,0:T(8,128)} %prev.1, bf16[2,64,1024]{2,1,0:T(8,128)(2,1)} %ham.1, f32[6,1024]{1,0:T(8,128)} %cv.1, f32[2,6]{1,0:T(2,128)} %coup.1, f32[6]{0:T(128)} %damp.1, s32[3,6]{1,0:T(4,128)} %occ.1, s32[8,128]{1,0:T(8,128)} %constant.4.clone.tab), custom_call_target="tpu_custom_call" | custom-call | tf_op jit(solution)/shard_map/section/pallas_call | solution.py:406
  67.1 0.0 copy-done.1
  67.1 0.0 copy-start
  67.1 3.0 %multiply_add_fusion = f32[3,2,64,1024]{3,2,1,0:T(8,128)} fusion(f32[3,2,64,1024]{3,2,1,0:T(8,128)S(1)} %copy-done.1, f32[3,2,64,1024]{3,2,1,0:T(8,128)} %section.1), kind=kLoop, calls=%fused_computation | loop fusion | flops 786432 | bytes 4718592 | tf_op jit(solution)/shard_map/add | solution.py:446
  70.1 0.0 copy-done
  70.1 1.1 %copy.12 = f32[3,2,64,1024]{3,2,1,0:T(8,128)} copy(f32[3,2,64,1024]{3,2,1,0:T(8,128)S(1)} %copy-done) | data formatting | bytes 3145728
Async XLA Ops:
  0.6 66.4 %copy-start.1 = (f32[3,2,64,1024]{3,2,1,0:T(8,128)S(1)}, f32[3,2,64,1024]{3,2,1,0:T(8,128)}, u32[]{:S(2)}) copy-start(f32[3,2,64,1024]{3,2,1,0:T(8,128)} %param.13) | copy-start | bytes 4718596
  67.1 3.0 %copy-start = (f32[3,2,64,1024]{3,2,1,0:T(8,128)S(1)}, f32[3,2,64,1024]{3,2,1,0:T(8,128)}, u32[]{:S(2)}) copy-start(f32[3,2,64,1024]{3,2,1,0:T(8,128)} %section.1) | copy-start | bytes 4718596
where the time goes:
time: 72.1 us; the launch traced here: 71.2 us
  Pallas kernels  66.4 us (92%)
  other arithmetic  2.96 us (4%)
  local copies, waits for them, and re-layouts  1.15 us (2%)
    pallas_call x1, Pallas kernels, shards(): pl.pallas_call(kernel, name='section', out_shape=jax.ShapeDtypeStruct((3,...  66.4 us
    add x1, other arithmetic, shards(): return (slope, accumulated + STEP / 3.0 * slope)  2.96 us

commit v1 on v0

v1 whole, which is shorter than its diff:
```python
import jax
import jax.numpy as jnp
import numpy as np
from jax import lax
from jax.experimental import pallas as pl
from jax.experimental.pallas import tpu as pltpu
from jax.sharding import PartitionSpec as P

MESH = pl.DeviceIdType.MESH
N = 1024
MODES = 6
ADOS = 48
STEP = 0.5
F32 = jnp.float32
BF16 = jnp.bfloat16


def window_table():
    entries = [()]
    for _ in range(MODES):
        entries = [entry + (level,) for entry in entries for level in range(5)]
    chosen = [entry for entry in entries if sum(entry) <= 4]
    return sorted(chosen, key=lambda entry: (sum(entry), entry))[:ADOS]


TABLE = window_table()
PLACE = {entry: place for place, entry in enumerate(TABLE)}


def key_of(entry):
    return sum(entry[k] * 5**k for k in range(MODES))


def shifted(entry, mode, by):
    return PLACE.get(entry[:mode] + (entry[mode] + by,) + entry[mode + 1 :])


def key_table():
    keys = np.full((8, 128), -1, np.int32)
    keys[:, :ADOS] = [key_of(entry) for entry in TABLE]
    return keys


R_HN = 0
R_HU = 1
R_HD = 3
R_H2 = 5
R_HP = 9
R_L = 17
R_LP = 25
R_LR = 33
R_M = 41
R_A = 57
R_C = 89
N_RECV = 121
N_SEND = 140


def kernel(
    state,
    prev,
    acc,
    ham,
    cv_in,
    coup_in,
    damp_in,
    occ_in,
    tab_in,
    slope,
    acc_out,
    st_v,
    pv_v,
    acc_v,
    cv,
    tab,
    coup,
    damp,
    occ,
    sblk,
    amat,
    hn,
    lb,
    lout,
    lret,
    zin_0,
    zin_1,
    ccan,
    cout,
    cret,
    rbuf,
    slope_v,
    meta_out,
    meta_in,
    meta_v,
    meta_s,
    vt,
    dk,
    dg,
    eg,
    lsem,
    ssem,
    rsem,
):
    h = lax.axis_index("hier")
    r = lax.axis_index("row")
    xh, z = lax.div(h, 8), lax.rem(h, 8)
    p, c = lax.div(r, 2), lax.rem(r, 2)
    xl, y = lax.div(p, 4), lax.rem(p, 4)
    oc = 1 - c
    zin = (zin_0, zin_1)

    def chip(dx, dy):
        return lax.rem(xl + dx, 2) * 4 + lax.rem(y + dy, 4)

    def rowdev(dx, dy):
        return (h, chip(dx, dy) * 2 + c)

    def hier(dx, dz):
        return lax.rem(xh + dx, 2), lax.rem(z + dz, 8)

    other_core = (h, p * 2 + oc)
    x_cross = ((1 - xh) * 8 + z, ((1 - xl) * 4 + y) * 2 + c)

    row_offsets = [(dx, dy) for dy in (2, 1, 3, 0) for dx in (1, 0) if dx or dy]
    hier_offsets = [(dx, dz) for dz in (4, 3, 5, 2, 6, 1, 7, 0) for dx in (1, 0) if dx or dz]

    cp_h = pltpu.make_async_copy(ham, hn.at[:, p, c], lsem.at[0])
    cp_s = pltpu.make_async_copy(state, st_v, lsem.at[1])
    cp_p = pltpu.make_async_copy(prev, pv_v, lsem.at[2])
    cp_s.start()
    cp_p.start()
    cp_h.start()
    small = []
    for i, (src, dst) in enumerate(
        [(occ_in, occ), (tab_in, tab), (cv_in, cv), (coup_in, coup), (damp_in, damp), (acc, acc_v)]
    ):
        small.append(pltpu.make_async_copy(src, dst, lsem.at[10 + i]))
        small[i].start()

    barrier = pltpu.get_barrier_semaphore()
    greeted = []
    for dx, dz in hier_offsets:
        hx, hz = hier(dx, dz)
        greeted.append((hx * 8 + hz, r))
    greeted += [rowdev(dx, dy) for dx, dy in row_offsets]
    greeted += [x_cross, other_core]
    for dev in greeted:
        pl.semaphore_signal(barrier, inc=1, device_id=dev, device_id_type=MESH)

    for copy in small[:2]:
        copy.wait()
    lane = lax.broadcasted_iota(jnp.int32, (8, 128), 1)
    line = lax.broadcasted_iota(jnp.int32, (8, 128), 0)
    slots = jnp.zeros((8, 128), jnp.int32)
    places = jnp.zeros((8, 128), jnp.int32)
    for j in range(3):
        key = occ[j, 0]
        for k in range(1, MODES):
            key = key + occ[j, k] * (5**k)
        hit = tab[...] == key
        slots = slots + jnp.where(hit, 3 * h + j, 0)
        place = jnp.sum(jnp.where(hit, lane, 0), axis=1, keepdims=True)
        places = places + jnp.where(lane == 3 * h + j, place, 0)
    mine = jnp.where(line == 0, slots, places)
    meta_out[...] = mine
    meta_in[h] = mine

    cp_s.wait()
    cp_p.wait()

    @pl.loop(0, 3)
    def _(a):
        for quarter in range(4):
            rows = pl.ds(16 * quarter, 16)
            for b in range(8):
                cols = pl.ds(128 * b, 128)
                parts = []
                for ri in range(2):
                    value = st_v[a, ri, rows, cols].astype(F32) + (0.5 * STEP) * pv_v[a, ri, rows, cols]
                    parts.append(value.astype(BF16))
                    sblk[b, quarter, a, ri] = parts[ri]
                    amat[quarter, a, ri, :, cols] = parts[ri]
                late = pl.ds(N + 128 * b, 128)
                amat[quarter, a, 0, :, late] = -parts[1]
                amat[quarter, a, 1, :, late] = parts[0]

    cp_h.wait()
    pl.semaphore_wait(barrier, len(greeted))

    sent = []

    def send(src, dst, to, dev):
        copy = pltpu.make_async_remote_copy(
            src_ref=src,
            dst_ref=dst,
            send_sem=ssem.at[len(sent)],
            recv_sem=rsem.at[to],
            device_id=dev,
            device_id_type=MESH,
        )
        copy.start()
        sent.append(copy)

    def arrived(dst, to):
        pltpu.make_async_remote_copy(
            src_ref=dst,
            dst_ref=dst,
            send_sem=ssem.at[0],
            recv_sem=rsem.at[to],
            device_id=other_core,
            device_id_type=MESH,
        ).wait_recv()

    def hblk(q):
        return hn.at[:, q, c]

    def send_h(q, to, dev):
        send(hblk(q), hblk(q), to, dev)

    send_h(p, R_HN, x_cross)
    send_h(p, R_HU, rowdev(0, 1))
    send_h(p, R_HD, rowdev(0, 3))
    for q in range(2):
        for dx, dz in hier_offsets:
            hx, hz = hier(dx, dz)
            dev = (hx * 8 + hz, r)
            if q == 0:
                send(meta_out, meta_in.at[h], R_M + 8 * dx + dz, dev)
            send(sblk.at[hz, 2 * hx + q], zin[q].at[pl.ds(3 * h, 3)], R_A + 16 * q + 8 * dx + dz, dev)
    for dx, dy in row_offsets:
        q = chip(dx, dy)
        send(sblk.at[q], lb.at[p, c], R_L + 4 * dx + dy, (h, q * 2 + c))
    send_h(p, R_HP, other_core)
    send(sblk.at[p], lb.at[p, c], R_LP, other_core)
    lb[p, c] = sblk[p]
    for q in range(2):
        zin[q][pl.ds(3 * h, 3)] = sblk[z, 2 * xh + q]

    for copy in small[2:]:
        copy.wait()
    for k in range(MODES):
        line_v = cv[pl.ds(k, 1), pl.ds(pl.multiple_of(128 * p, 128), 128)]
        vt[k] = jnp.broadcast_to(line_v, (128, 128)).T
        v_rows = vt[k, pl.ds(pl.multiple_of(64 * c + 32 * xh, 32), 32), :]
        v_cols = cv[pl.ds(k, 1), pl.ds(pl.multiple_of(128 * z, 128), 128)]
        diff = v_rows - v_cols
        dk[k] = diff
        dg[k] = coup[0, k] * diff
        eg[k] = coup[1, k] * (v_rows + v_cols)

    q = chip(1, 0)
    arrived(hblk(q), R_HN)
    send_h(q, R_HU + 1, rowdev(0, 1))
    send_h(q, R_HD + 1, rowdev(0, 3))
    send_h(q, R_HP + 4, other_core)

    def pass_on_h(dx):
        below, above = chip(dx, 3), chip(dx, 1)
        arrived(hblk(below), R_HU + dx)
        send(hn.at[0, below, c], hn.at[0, below, c], R_H2 + 2 * dx, rowdev(0, 1))
        arrived(hblk(above), R_HD + dx)
        send(hn.at[1, above, c], hn.at[1, above, c], R_H2 + 2 * dx + 1, rowdev(0, 3))
        send_h(below, R_HP + 4 * dx + 3, other_core)
        send_h(above, R_HP + 4 * dx + 1, other_core)

    pass_on_h(0)

    for dx, dz in hier_offsets:
        hx, hz = hier(dx, 8 - dz)
        arrived(meta_in.at[hx * 8 + hz], R_M + 8 * dx + dz)
    meta_v[...] = jnp.minimum(jnp.sum(meta_in[...], axis=0), ADOS - 1)
    cp_m = pltpu.make_async_copy(meta_v, meta_s, lsem.at[3])
    cp_m.start()
    cp_m.wait()

    def couple(q):
        for dx, dz in hier_offsets:
            hx, hz = hier(dx, 8 - dz)
            arrived(zin[q].at[pl.ds(3 * (hx * 8 + hz), 3)], R_A + 16 * q + 8 * dx + dz)
        rows = pl.ds(16 * q, 16)
        for place, entry in enumerate(TABLE):
            re = jnp.zeros((16, 128), F32)
            im = jnp.zeros((16, 128), F32)
            for k in range(MODES):
                child = shifted(entry, k, 1)
                if child is not None:
                    near = zin[q][meta_s[0, child]].astype(F32)
                    re = re + dk[k, rows] * near[1]
                    im = im - dk[k, rows] * near[0]
                if entry[k] > 0:
                    near = zin[q][meta_s[0, shifted(entry, k, -1)]].astype(F32)
                    add_re = dg[k, rows] * near[1] + eg[k, rows] * near[0]
                    add_im = eg[k, rows] * near[1] - dg[k, rows] * near[0]
                    if entry[k] > 1:
                        add_re = add_re * float(entry[k])
                        add_im = add_im * float(entry[k])
                    re = re + add_re
                    im = im + add_im
            ccan[place, 0] = re.astype(BF16)
            ccan[place, 1] = im.astype(BF16)
        for slot in range(ADOS):
            cout[q, slot] = ccan[meta_s[1, slot]]
        for dx, dz in hier_offsets:
            hx, hz = hier(dx, dz)
            to = hx * 8 + hz
            send(cout.at[q, pl.ds(3 * to, 3)], cret.at[2 * xh + q, z], R_C + 16 * q + 8 * dx + dz, (to, r))
        cret[2 * xh + q, z] = cout[q, pl.ds(3 * h, 3)]

    pass_on_h(1)
    couple(0)

    for dx, dy in row_offsets[2:] + row_offsets[:2]:
        back = (4 - dy) % 4
        q = chip(dx, back)
        arrived(lb.at[q, c], R_L + 4 * dx + dy)
        send(lb.at[q, c], lb.at[q, c], R_LP + 4 * dx + back, other_core)
    for dx in range(2):
        q = chip(dx, 2)
        arrived(hn.at[0, q, c], R_H2 + 2 * dx)
        arrived(hn.at[1, q, c], R_H2 + 2 * dx + 1)
        send_h(q, R_HP + 4 * dx + 2, other_core)

    couple(1)

    for dx in range(2):
        for dy in range(4):
            arrived(lb.at[chip(dx, dy), oc], R_LP + 4 * dx + dy)

    @pl.loop(0, 3)
    def _(a):
        real = lb[:, :, :, a, 0].reshape(N, 128)
        imag = lb[:, :, :, a, 1].reshape(N, 128)
        rhs = jnp.concatenate(
            [jnp.concatenate([real, imag], 1), jnp.concatenate([-imag, real], 1)], 0
        )
        for m in range(2):
            lhs = jnp.concatenate(
                [hn[ri, pl.ds(4 * m, 4), c].reshape(256, N) for ri in range(2)], 1
            )
            out = jnp.dot(lhs, rhs, preferred_element_type=F32).astype(BF16)
            out = out.reshape(4, 4, 16, 256)
            lout[pl.ds(4 * m, 4), :, a, 0] = out[..., :128]
            lout[pl.ds(4 * m, 4), :, a, 1] = out[..., 128:]

    for dx, dy in row_offsets:
        q = chip(dx, dy)
        send(lout.at[q], lret.at[p], R_LR + 4 * dx + dy, (h, q * 2 + c))
    lret[p] = lout[p]

    for dx in range(2):
        for dy in range(4):
            arrived(hn.at[:, chip(dx, dy), oc], R_HP + 4 * dx + dy)

    @pl.loop(0, 4)
    def _(n):
        cols = pl.ds(pl.multiple_of(256 * n, 256), 256)
        rhs = jnp.concatenate(
            [hn[ri, :, :, :, cols].reshape(N, 256) for ri in range(2)], 0
        )
        lhs = amat[...].reshape(384, 2 * N)
        out = jnp.dot(lhs, rhs, preferred_element_type=F32)
        rbuf[:, :, :, :, cols] = out.reshape(4, 3, 2, 16, 256)

    for q in range(2):
        for dx, dz in hier_offsets:
            hx, hz = hier(dx, 8 - dz)
            arrived(cret.at[2 * hx + q, hz], R_C + 16 * q + 8 * dx + dz)
    for dx, dy in row_offsets:
        back = (4 - dy) % 4
        arrived(lret.at[chip(dx, back)], R_LR + 4 * dx + dy)

    @pl.loop(0, 3)
    def _(a):
        decay = occ[a, 0].astype(F32) * damp[0]
        for k in range(1, MODES):
            decay = decay + occ[a, k].astype(F32) * damp[k]
        for quarter in range(4):
            for b in range(8):
                cols = pl.ds(128 * b, 128)
                for ri in range(2):
                    turned = lret[b, quarter, a, 1 - ri].astype(F32) - rbuf[quarter, a, 1 - ri, :, cols]
                    if ri:
                        turned = -turned
                    value = turned - decay * sblk[b, quarter, a, ri].astype(F32)
                    value = value + cret[quarter, b, a, ri].astype(F32)
                    rows = pl.ds(16 * quarter, 16)
                    slope_v[a, ri, rows, cols] = value
                    pv_v[a, ri, rows, cols] = acc_v[a, ri, rows, cols] + (STEP / 3.0) * value
        pltpu.make_async_copy(slope_v.at[a], slope.at[a], lsem.at[4 + a]).start()
        pltpu.make_async_copy(pv_v.at[a], acc_out.at[a], lsem.at[7 + a]).start()

    for a in range(3):
        pltpu.make_async_copy(slope_v.at[a], slope.at[a], lsem.at[4 + a]).wait()
        pltpu.make_async_copy(pv_v.at[a], acc_out.at[a], lsem.at[7 + a]).wait()
    for copy in sent:
        copy.wait_send()


def shards(state, prev_slope, accumulated, hamiltonian, couple_v, coupling, damping, occupation, parents, children):
    vmem = pltpu.VMEM
    anywhere = pl.BlockSpec(memory_space=pl.ANY)
    block = jax.ShapeDtypeStruct((3, 2, 64, N), F32)
    return pl.pallas_call(
        kernel,
        name="section",
        out_shape=(block, block),
        in_specs=[anywhere] * 9,
        out_specs=(anywhere, anywhere),
        scratch_shapes=[
            vmem((3, 2, 64, N), BF16),
            vmem((3, 2, 64, N), F32),
            vmem((3, 2, 64, N), F32),
            vmem((MODES, N), F32),
            vmem((8, 128), jnp.int32),
            pltpu.SMEM((2, MODES), F32),
            pltpu.SMEM((MODES,), F32),
            pltpu.SMEM((3, MODES), jnp.int32),
            vmem((8, 4, 3, 2, 16, 128), BF16),
            vmem((4, 3, 2, 16, 2 * N), BF16),
            vmem((2, 8, 2, 64, N), BF16),
            vmem((8, 2, 4, 3, 2, 16, 128), BF16),
            vmem((8, 4, 3, 2, 16, 128), BF16),
            vmem((8, 4, 3, 2, 16, 128), BF16),
            vmem((ADOS, 2, 16, 128), BF16),
            vmem((ADOS, 2, 16, 128), BF16),
            vmem((ADOS, 2, 16, 128), BF16),
            vmem((2, ADOS, 2, 16, 128), BF16),
            vmem((4, 8, 3, 2, 16, 128), BF16),
            vmem((4, 3, 2, 16, N), F32),
            vmem((3, 2, 64, N), F32),
            vmem((8, 128), jnp.int32),
            vmem((16, 8, 128), jnp.int32),
            vmem((8, 128), jnp.int32),
            pltpu.SMEM((8, 128), jnp.int32),
            vmem((MODES, 128, 128), F32),
            vmem((MODES, 32, 128), F32),
            vmem((MODES, 32, 128), F32),
            vmem((MODES, 32, 128), F32),
            pltpu.SemaphoreType.DMA((16,)),
            pltpu.SemaphoreType.DMA((N_SEND,)),
            pltpu.SemaphoreType.DMA((N_RECV,)),
        ],
        compiler_params=pltpu.CompilerParams(collective_id=0, has_side_effects=True),
    )(
        state,
        prev_slope,
        accumulated,
        hamiltonian,
        couple_v,
        coupling,
        damping,
        occupation,
        jnp.asarray(key_table()),
    )


def solution(mesh):
    block = P("hier", None, "row", None)
    return jax.shard_map(
        shards,
        mesh=mesh,
        in_specs=(
            block,
            block,
            block,
            P(None, "row", None),
            P(),
            P(),
            P(),
            P("hier", None),
            P("hier", None),
            P("hier", None),
        ),
        out_specs=(block, block),
        check_vma=False,
    )
```

time: 72.1 us -> 63.3 us (0.88)
  the two profiles are of different devices: /device:TPU:24 before, /device:TPU:2 now
where the time goes in v1:
time: 63.3 us; the launch traced here: 63.2 us
  Pallas kernels  58.5 us (92%)
  local copies, waits for them, and re-layouts  3.99 us (6%)
  between operations  0.65 us (1%)
    pallas_call x1, Pallas kernels, shards(): pl.pallas_call(kernel, name='section', out_shape=(block, block), in_specs...  58.5 us
    unnamed x4, local copies, waits for them, and re-layouts  3.99 us

profile of v1, /device:TPU:2, one launch (start us, length us, event | category | flops | bytes accessed | tf_op | source)
XLA Modules:
  0.0 63.2 jit_solution(4686708623133021810)
XLA Ops:
  0.6 58.5 %section.1 = (f32[3,2,64,1024]{3,2,1,0:T(8,128)}, f32[3,2,64,1024]{3,2,1,0:T(8,128)}) custom-call(bf16[3,2,64,1024]{3,2,1,0:T(8,128)(2,1)} %state.1, f32[3,2,64,1024]{3,2,1,0:T(8,128)} %prev.1, f32[3,2,64,1024]{3,2,1,0:T(8,128)} %acc.1, bf16[2,64,1024]{2,1,0:T(8,128)(2,1)} %ham.1, f32[6,1024]{1,0:T(8,128)} %cv_in.1, f32[2,6]{1,0:T(2,128)} %coup_in.1, ...), custom_call_target="tpu_custom_call" | custom-call | tf_op jit(solution)/shard_map/section/pallas_call | solution.py:403
  59.2 0.0 copy-start
  59.2 2.8 %copy.13 = f32[3,2,64,1024]{3,2,1,0:T(8,128)} copy(f32[3,2,64,1024]{3,2,1,0:T(8,128)} %get-tuple-element.4) | data formatting | bytes 3145728
  62.0 0.0 copy-done
  62.0 1.1 %copy.14 = f32[3,2,64,1024]{3,2,1,0:T(8,128)} copy(f32[3,2,64,1024]{3,2,1,0:T(8,128)S(1)} %copy-done) | data formatting | bytes 3145728
Async XLA Ops:
  59.2 2.9 %copy-start = (f32[3,2,64,1024]{3,2,1,0:T(8,128)S(1)}, f32[3,2,64,1024]{3,2,1,0:T(8,128)}, u32[]{:S(2)}) copy-start(f32[3,2,64,1024]{3,2,1,0:T(8,128)} %get-tuple-element.5) | copy-start | bytes 4718596

commit v2 on v1

--- a/solution.py
+++ b/solution.py
@@ -78,6 +78,8 @@
     occ,
     sblk,
     amat,
+    hv,
+    mb,
     hn,
     lb,
     lout,
@@ -124,7 +126,7 @@
     row_offsets = [(dx, dy) for dy in (2, 1, 3, 0) for dx in (1, 0) if dx or dy]
     hier_offsets = [(dx, dz) for dz in (4, 3, 5, 2, 6, 1, 7, 0) for dx in (1, 0) if dx or dz]
 
-    cp_h = pltpu.make_async_copy(ham, hn.at[:, p, c], lsem.at[0])
+    cp_h = pltpu.make_async_copy(ham, hv, lsem.at[0])
     cp_s = pltpu.make_async_copy(state, st_v, lsem.at[1])
     cp_p = pltpu.make_async_copy(prev, pv_v, lsem.at[2])
     cp_s.start()
@@ -185,6 +187,10 @@
                 amat[quarter, a, 1, :, late] = parts[0]
 
     cp_h.wait()
+    across = lax.broadcasted_iota(jnp.int32, (64, N), 1)
+    down = lax.broadcasted_iota(jnp.int32, (64, N), 0) + 64 * r
+    mb[p, c] = jnp.where(across >= down, hv[0].astype(F32), hv[1].astype(F32)).astype(BF16)
+
     pl.semaphore_wait(barrier, len(greeted))
 
     sent = []
@@ -212,25 +218,38 @@
         ).wait_recv()
 
     def hblk(q):
-        return hn.at[:, q, c]
+        return mb.at[q, c]
 
     def send_h(q, to, dev):
         send(hblk(q), hblk(q), to, dev)
 
-    send_h(p, R_HN, x_cross)
-    send_h(p, R_HU, rowdev(0, 1))
-    send_h(p, R_HD, rowdev(0, 3))
-    for q in range(2):
+    def send_section(q):
         for dx, dz in hier_offsets:
             hx, hz = hier(dx, dz)
             dev = (hx * 8 + hz, r)
             if q == 0:
                 send(meta_out, meta_in.at[h], R_M + 8 * dx + dz, dev)
             send(sblk.at[hz, 2 * hx + q], zin[q].at[pl.ds(3 * h, 3)], R_A + 16 * q + 8 * dx + dz, dev)
-    for dx, dy in row_offsets:
-        q = chip(dx, dy)
-        send(sblk.at[q], lb.at[p, c], R_L + 4 * dx + dy, (h, q * 2 + c))
+
+    def send_columns(way):
+        for dx, dy in row_offsets:
+            if dx == way:
+                q = chip(dx, dy)
+                send(sblk.at[q], lb.at[p, c], R_L + 4 * dx + dy, (h, q * 2 + c))
+
+    send_h(p, R_HN, x_cross)
+    send_h(p, R_HU, rowdev(0, 1))
+    send_h(p, R_HD, rowdev(0, 3))
+    send_section(0)
     send_h(p, R_HP, other_core)
+
+    q = chip(1, 0)
+    arrived(hblk(q), R_HN)
+    send_h(q, R_HU + 1, rowdev(0, 1))
+    send_h(q, R_HD + 1, rowdev(0, 3))
+    send_columns(1)
+    send_section(1)
+    send_h(q, R_HP + 4, other_core)
     send(sblk.at[p], lb.at[p, c], R_LP, other_core)
     lb[p, c] = sblk[p]
     for q in range(2):
@@ -248,22 +267,23 @@
         dg[k] = coup[0, k] * diff
         eg[k] = coup[1, k] * (v_rows + v_cols)
 
-    q = chip(1, 0)
-    arrived(hblk(q), R_HN)
-    send_h(q, R_HU + 1, rowdev(0, 1))
-    send_h(q, R_HD + 1, rowdev(0, 3))
-    send_h(q, R_HP + 4, other_core)
-
-    def pass_on_h(dx):
+    def half_h(q, half):
+        return mb.at[q, c, pl.ds(32 * half, 32)]
+
+    for dx in range(2):
         below, above = chip(dx, 3), chip(dx, 1)
         arrived(hblk(below), R_HU + dx)
-        send(hn.at[0, below, c], hn.at[0, below, c], R_H2 + 2 * dx, rowdev(0, 1))
+        send(half_h(below, 0), half_h(below, 0), R_H2 + 2 * dx, rowdev(0, 1))
         arrived(hblk(above), R_HD + dx)
-        send(hn.at[1, above, c], hn.at[1, above, c], R_H2 + 2 * dx + 1, rowdev(0, 3))
+        send(half_h(above, 1), half_h(above, 1), R_H2 + 2 * dx + 1, rowdev(0, 3))
         send_h(below, R_HP + 4 * dx + 3, other_core)
         send_h(above, R_HP + 4 * dx + 1, other_core)
-
-    pass_on_h(0)
+    send_columns(0)
+    for dx in range(2):
+        q = chip(dx, 2)
+        arrived(half_h(q, 0), R_H2 + 2 * dx)
+        arrived(half_h(q, 1), R_H2 + 2 * dx + 1)
+        send_h(q, R_HP + 4 * dx + 2, other_core)
 
     for dx, dz in hier_offsets:
         hx, hz = hier(dx, 8 - dz)
@@ -306,19 +326,38 @@
             send(cout.at[q, pl.ds(3 * to, 3)], cret.at[2 * xh + q, z], R_C + 16 * q + 8 * dx + dz, (to, r))
         cret[2 * xh + q, z] = cout[q, pl.ds(3 * h, 3)]
 
-    pass_on_h(1)
     couple(0)
 
-    for dx, dy in row_offsets[2:] + row_offsets[:2]:
+    for dx in range(2):
+        for dy in range(4):
+            arrived(mb.at[chip(dx, dy), oc], R_HP + 4 * dx + dy)
+    under = lax.broadcasted_iota(jnp.int32, (128, 128), 0)
+    along = lax.broadcasted_iota(jnp.int32, (128, 128), 1)
+
+    def put(ri, i, j, tile):
+        hn[ri, i, :, :, pl.ds(128 * j, 128)] = tile.reshape(2, 64, 128)
+
+    for i in range(8):
+        for j in range(i, 8):
+            upper = mb[i, :, :, pl.ds(128 * j, 128)].reshape(128, 128)
+            if i == j:
+                wide = upper.astype(F32)
+                flipped = wide.T
+                put(0, i, i, jnp.where(along >= under, wide, flipped).astype(BF16))
+                below = jnp.where(along > under, -flipped, 0.0)
+                put(1, i, i, jnp.where(along < under, wide, below).astype(BF16))
+            else:
+                lower = mb[j, :, :, pl.ds(128 * i, 128)].reshape(128, 128)
+                put(0, i, j, upper)
+                put(0, j, i, upper.T)
+                put(1, i, j, -lower.T)
+                put(1, j, i, lower)
+
+    for dx, dy in row_offsets:
         back = (4 - dy) % 4
         q = chip(dx, back)
         arrived(lb.at[q, c], R_L + 4 * dx + dy)
         send(lb.at[q, c], lb.at[q, c], R_LP + 4 * dx + back, other_core)
-    for dx in range(2):
-        q = chip(dx, 2)
-        arrived(hn.at[0, q, c], R_H2 + 2 * dx)
-        arrived(hn.at[1, q, c], R_H2 + 2 * dx + 1)
-        send_h(q, R_HP + 4 * dx + 2, other_core)
 
     couple(1)
 
@@ -346,10 +385,6 @@
         q = chip(dx, dy)
         send(lout.at[q], lret.at[p], R_LR + 4 * dx + dy, (h, q * 2 + c))
     lret[p] = lout[p]
-
-    for dx in range(2):
-        for dy in range(4):
-            arrived(hn.at[:, chip(dx, dy), oc], R_HP + 4 * dx + dy)
 
     @pl.loop(0, 4)
     def _(n):
@@ -417,6 +452,8 @@
             pltpu.SMEM((3, MODES), jnp.int32),
             vmem((8, 4, 3, 2, 16, 128), BF16),
             vmem((4, 3, 2, 16, 2 * N), BF16),
+            vmem((2, 64, N), BF16),
+            vmem((8, 2, 64, N), BF16),
             vmem((2, 8, 2, 64, N), BF16),
             vmem((8, 2, 4, 3, 2, 16, 128), BF16),
             vmem((8, 4, 3, 2, 16, 128), BF16),

time: 63.3 us -> 60.2 us (0.951)
  the two profiles are of different devices: /device:TPU:2 before, /device:TPU:24 now
where the time goes in v2:
time: 60.2 us; the launch traced here: 60.1 us
  Pallas kernels  55.4 us (92%)
  local copies, waits for them, and re-layouts  3.99 us (7%)
  between operations  0.65 us (1%)
    pallas_call x1, Pallas kernels, shards(): pl.pallas_call(kernel, name='section', out_shape=(block, block), in_specs...  55.4 us
    unnamed x4, local copies, waits for them, and re-layouts  3.99 us

profile of v2, /device:TPU:24, one launch (start us, length us, event | category | flops | bytes accessed | tf_op | source)
XLA Modules:
  0.0 60.1 jit_solution(4990432911201234386)
XLA Ops:
  0.6 55.4 %section.1 = (f32[3,2,64,1024]{3,2,1,0:T(8,128)}, f32[3,2,64,1024]{3,2,1,0:T(8,128)}) custom-call(bf16[3,2,64,1024]{3,2,1,0:T(8,128)(2,1)} %state.1, f32[3,2,64,1024]{3,2,1,0:T(8,128)} %prev.1, f32[3,2,64,1024]{3,2,1,0:T(8,128)} %acc.1, bf16[2,64,1024]{2,1,0:T(8,128)(2,1)} %ham.1, f32[6,1024]{1,0:T(8,128)} %cv_in.1, f32[2,6]{1,0:T(2,128)} %coup_in.1, ...), custom_call_target="tpu_custom_call" | custom-call | tf_op jit(solution)/shard_map/section/pallas_call | solution.py:438
  56.1 0.0 copy-start
  56.1 2.8 %copy.13 = f32[3,2,64,1024]{3,2,1,0:T(8,128)} copy(f32[3,2,64,1024]{3,2,1,0:T(8,128)} %get-tuple-element.4) | data formatting | bytes 3145728
  58.9 0.0 copy-done
  58.9 1.1 %copy.14 = f32[3,2,64,1024]{3,2,1,0:T(8,128)} copy(f32[3,2,64,1024]{3,2,1,0:T(8,128)S(1)} %copy-done) | data formatting | bytes 3145728
Async XLA Ops:
  56.1 2.9 %copy-start = (f32[3,2,64,1024]{3,2,1,0:T(8,128)S(1)}, f32[3,2,64,1024]{3,2,1,0:T(8,128)}, u32[]{:S(2)}) copy-start(f32[3,2,64,1024]{3,2,1,0:T(8,128)} %get-tuple-element.5) | copy-start | bytes 4718596

commit v3 on v2

--- a/solution.py
+++ b/solution.py
@@ -90,7 +90,6 @@
     cout,
     cret,
     rbuf,
-    slope_v,
     meta_out,
     meta_in,
     meta_v,
@@ -419,14 +418,9 @@
                     value = turned - decay * sblk[b, quarter, a, ri].astype(F32)
                     value = value + cret[quarter, b, a, ri].astype(F32)
                     rows = pl.ds(16 * quarter, 16)
-                    slope_v[a, ri, rows, cols] = value
-                    pv_v[a, ri, rows, cols] = acc_v[a, ri, rows, cols] + (STEP / 3.0) * value
-        pltpu.make_async_copy(slope_v.at[a], slope.at[a], lsem.at[4 + a]).start()
-        pltpu.make_async_copy(pv_v.at[a], acc_out.at[a], lsem.at[7 + a]).start()
-
-    for a in range(3):
-        pltpu.make_async_copy(slope_v.at[a], slope.at[a], lsem.at[4 + a]).wait()
-        pltpu.make_async_copy(pv_v.at[a], acc_out.at[a], lsem.at[7 + a]).wait()
+                    slope[a, ri, rows, cols] = value
+                    acc_out[a, ri, rows, cols] = acc_v[a, ri, rows, cols] + (STEP / 3.0) * value
+
     for copy in sent:
         copy.wait_send()
 
@@ -434,13 +428,14 @@
 def shards(state, prev_slope, accumulated, hamiltonian, couple_v, coupling, damping, occupation, parents, children):
     vmem = pltpu.VMEM
     anywhere = pl.BlockSpec(memory_space=pl.ANY)
-    block = jax.ShapeDtypeStruct((3, 2, 64, N), F32)
+    in_vmem = pl.BlockSpec(memory_space=pltpu.VMEM)
+    block = vmem((3, 2, 64, N), F32)
     return pl.pallas_call(
         kernel,
         name="section",
         out_shape=(block, block),
         in_specs=[anywhere] * 9,
-        out_specs=(anywhere, anywhere),
+        out_specs=(in_vmem, in_vmem),
         scratch_shapes=[
             vmem((3, 2, 64, N), BF16),
             vmem((3, 2, 64, N), F32),
@@ -464,7 +459,6 @@
             vmem((2, ADOS, 2, 16, 128), BF16),
             vmem((4, 8, 3, 2, 16, 128), BF16),
             vmem((4, 3, 2, 16, N), F32),
-            vmem((3, 2, 64, N), F32),
             vmem((8, 128), jnp.int32),
             vmem((16, 8, 128), jnp.int32),
             vmem((8, 128), jnp.int32),

time: 60.2 us -> 57.2 us (0.950)
  local copies, waits for them, and re-layouts: 3.99 us -> 2.29 us
  Pallas kernels: 55.4 us -> 54.1 us
    unnamed x4 -> x2, local copies, waits for them, and re-layouts: 3.99 us -> 2.29 us
    pallas_call x1, Pallas kernels: 55.4 us -> 54.1 us  [shards(): pl.pallas_call(kernel, name='section', out_shape=(block, block), in_specs...]
where the time goes in v3:
time: 57.2 us; the launch traced here: 57.1 us
  Pallas kernels  54.1 us (95%)
  local copies, waits for them, and re-layouts  2.29 us (4%)
  between operations  0.64 us (1%)
    pallas_call x1, Pallas kernels, shards(): pl.pallas_call(kernel, name='section', out_shape=(block, block), in_specs...  54.1 us
    unnamed x2, local copies, waits for them, and re-layouts  2.29 us

profile of v3, /device:TPU:24, one launch (start us, length us, event | category | flops | bytes accessed | tf_op | source)
XLA Modules:
  0.0 57.1 jit_solution(14443441812092009188)
XLA Ops:
  0.6 54.1 %section.1 = (f32[3,2,64,1024]{3,2,1,0:T(8,128)S(1)}, f32[3,2,64,1024]{3,2,1,0:T(8,128)S(1)}) custom-call(bf16[3,2,64,1024]{3,2,1,0:T(8,128)(2,1)} %state.1, f32[3,2,64,1024]{3,2,1,0:T(8,128)} %prev.1, f32[3,2,64,1024]{3,2,1,0:T(8,128)} %acc.1, bf16[2,64,1024]{2,1,0:T(8,128)(2,1)} %ham.1, f32[6,1024]{1,0:T(8,128)} %cv_in.1, f32[2,6]{1,0:T(2,128)} %coup_in.1, ...), custom_call_target="tpu_custom_call" | custom-call | tf_op jit(solution)/shard_map/section/pallas_call | solution.py:433
  54.8 1.1 %copy.13 = f32[3,2,64,1024]{3,2,1,0:T(8,128)} copy(f32[3,2,64,1024]{3,2,1,0:T(8,128)S(1)} %get-tuple-element.2) | data formatting | bytes 3145728
  55.9 1.1 %copy.14 = f32[3,2,64,1024]{3,2,1,0:T(8,128)} copy(f32[3,2,64,1024]{3,2,1,0:T(8,128)S(1)} %get-tuple-element.3) | data formatting | bytes 3145728

commit v4 on v3

--- a/solution.py
+++ b/solution.py
@@ -327,6 +327,12 @@
 
     couple(0)
 
+    for dx, dy in row_offsets:
+        back = (4 - dy) % 4
+        q = chip(dx, back)
+        arrived(lb.at[q, c], R_L + 4 * dx + dy)
+        send(lb.at[q, c], lb.at[q, c], R_LP + 4 * dx + back, other_core)
+
     for dx in range(2):
         for dy in range(4):
             arrived(mb.at[chip(dx, dy), oc], R_HP + 4 * dx + dy)
@@ -352,11 +358,6 @@
                 put(1, i, j, -lower.T)
                 put(1, j, i, lower)
 
-    for dx, dy in row_offsets:
-        back = (4 - dy) % 4
-        q = chip(dx, back)
-        arrived(lb.at[q, c], R_L + 4 * dx + dy)
-        send(lb.at[q, c], lb.at[q, c], R_LP + 4 * dx + back, other_core)
 
     couple(1)
 
@@ -425,12 +426,23 @@
         copy.wait_send()
 
 
+def leave(slope, acc, slope_out, acc_out, sem):
+    copies = []
+    for a in range(3):
+        for ri in range(2):
+            for src, dst in ((slope, slope_out), (acc, acc_out)):
+                copies.append(pltpu.make_async_copy(src.at[a, ri], dst.at[a, ri], sem.at[len(copies)]))
+                copies[-1].start()
+    for copy in copies:
+        copy.wait()
+
+
 def shards(state, prev_slope, accumulated, hamiltonian, couple_v, coupling, damping, occupation, parents, children):
     vmem = pltpu.VMEM
     anywhere = pl.BlockSpec(memory_space=pl.ANY)
     in_vmem = pl.BlockSpec(memory_space=pltpu.VMEM)
     block = vmem((3, 2, 64, N), F32)
-    return pl.pallas_call(
+    results = pl.pallas_call(
         kernel,
         name="section",
         out_shape=(block, block),
@@ -483,6 +495,16 @@
         occupation,
         jnp.asarray(key_table()),
     )
+    whole = jax.ShapeDtypeStruct((3, 2, 64, N), F32)
+    return pl.pallas_call(
+        leave,
+        name="leave",
+        out_shape=(whole, whole),
+        in_specs=[in_vmem, in_vmem],
+        out_specs=(anywhere, anywhere),
+        scratch_shapes=[pltpu.SemaphoreType.DMA((12,))],
+        compiler_params=pltpu.CompilerParams(vmem_limit_bytes=1 << 20),
+    )(*results)
 
 
 def solution(mesh):

time: 57.2 us -> 56.6 us (0.990)
  local copies, waits for them, and re-layouts: 2.29 us -> 0 us
  Pallas kernels: 54.1 us -> 55.9 us
    unnamed x2 -> x0, local copies, waits for them, and re-layouts: 2.29 us -> none
    pallas_call x0 -> x1, Pallas kernels: none -> 1.76 us  [shards(): pl.pallas_call(leave, name='leave', out_shape=(whole, whole), in_specs=[i...]
where the time goes in v4:
time: 56.6 us
  Pallas kernels  55.9 us (99%)
  between operations  0.64 us (1%)
    pallas_call x1, Pallas kernels, shards(): pl.pallas_call(kernel, name='section', out_shape=(block, block), in_specs...  54.2 us
    pallas_call x1, Pallas kernels, shards(): pl.pallas_call(leave, name='leave', out_shape=(whole, whole), in_specs=[i...  1.76 us

profile of v4, /device:TPU:24, one launch (start us, length us, event | category | flops | bytes accessed | tf_op | source)
XLA Modules:
  0.0 56.6 jit_solution(3982015120620117800)
XLA Ops:
  0.6 54.2 %section.1 = (f32[3,2,64,1024]{3,2,1,0:T(8,128)S(1)}, f32[3,2,64,1024]{3,2,1,0:T(8,128)S(1)}) custom-call(bf16[3,2,64,1024]{3,2,1,0:T(8,128)(2,1)} %state.1, f32[3,2,64,1024]{3,2,1,0:T(8,128)} %prev.1, f32[3,2,64,1024]{3,2,1,0:T(8,128)} %acc.1, bf16[2,64,1024]{2,1,0:T(8,128)(2,1)} %ham.1, f32[6,1024]{1,0:T(8,128)} %cv_in.1, f32[2,6]{1,0:T(2,128)} %coup_in.1, ...), custom_call_target="tpu_custom_call" | custom-call | tf_op jit(solution)/shard_map/section/pallas_call | solution.py:445
  54.8 1.8 %leave.1 = (f32[3,2,64,1024]{3,2,1,0:T(8,128)}, f32[3,2,64,1024]{3,2,1,0:T(8,128)}) custom-call(f32[3,2,64,1024]{3,2,1,0:T(8,128)S(1)} %get-tuple-element.4.slope, f32[3,2,64,1024]{3,2,1,0:T(8,128)S(1)} %get-tuple-element.5.acc), custom_call_target="tpu_custom_call" | custom-call | tf_op jit(solution)/shard_map/leave/pallas_call | solution.py:499

commit v5 on v4

--- a/solution.py
+++ b/solution.py
@@ -48,11 +48,11 @@
 R_HP = 9
 R_L = 17
 R_LP = 25
-R_LR = 33
 R_M = 41
 R_A = 57
 R_C = 89
-N_RECV = 121
+R_LR = 121
+N_RECV = 145
 N_SEND = 140
 
 
@@ -365,8 +365,7 @@
         for dy in range(4):
             arrived(lb.at[chip(dx, dy), oc], R_LP + 4 * dx + dy)
 
-    @pl.loop(0, 3)
-    def _(a):
+    for a in range(3):
         real = lb[:, :, :, a, 0].reshape(N, 128)
         imag = lb[:, :, :, a, 1].reshape(N, 128)
         rhs = jnp.concatenate(
@@ -380,10 +379,9 @@
             out = out.reshape(4, 4, 16, 256)
             lout[pl.ds(4 * m, 4), :, a, 0] = out[..., :128]
             lout[pl.ds(4 * m, 4), :, a, 1] = out[..., 128:]
-
-    for dx, dy in row_offsets:
-        q = chip(dx, dy)
-        send(lout.at[q], lret.at[p], R_LR + 4 * dx + dy, (h, q * 2 + c))
+        for dx, dy in row_offsets:
+            q = chip(dx, dy)
+            send(lout.at[q, :, a], lret.at[p, :, a], R_LR + 8 * a + 4 * dx + dy, (h, q * 2 + c))
     lret[p] = lout[p]
 
     @pl.loop(0, 4)
@@ -402,7 +400,8 @@
             arrived(cret.at[2 * hx + q, hz], R_C + 16 * q + 8 * dx + dz)
     for dx, dy in row_offsets:
         back = (4 - dy) % 4
-        arrived(lret.at[chip(dx, back)], R_LR + 4 * dx + dy)
+        for a in range(3):
+            arrived(lret.at[chip(dx, back), :, a], R_LR + 8 * a + 4 * dx + dy)
 
     @pl.loop(0, 3)
     def _(a):

time: 56.6 us -> 56.9 us (level); the launches traced: 56.6 us -> 56 us
  no operation moved by 1% of the time
where the time goes in v5:
time: 56.9 us; the launch traced here: 56 us
  Pallas kernels  55.4 us (97%)
  between operations  0.64 us (1%)
    pallas_call x1, Pallas kernels, shards(): pl.pallas_call(kernel, name='section', out_shape=(block, block), in_specs...  53.6 us
    pallas_call x1, Pallas kernels, shards(): pl.pallas_call(leave, name='leave', out_shape=(whole, whole), in_specs=[i...  1.76 us

profile of v5, /device:TPU:24, one launch (start us, length us, event | category | flops | bytes accessed | tf_op | source)
XLA Modules:
  0.0 56.0 jit_solution(5734273647397549201)
XLA Ops:
  0.6 53.6 %section.1 = (f32[3,2,64,1024]{3,2,1,0:T(8,128)S(1)}, f32[3,2,64,1024]{3,2,1,0:T(8,128)S(1)}) custom-call(bf16[3,2,64,1024]{3,2,1,0:T(8,128)(2,1)} %state.1, f32[3,2,64,1024]{3,2,1,0:T(8,128)} %prev.1, f32[3,2,64,1024]{3,2,1,0:T(8,128)} %acc.1, bf16[2,64,1024]{2,1,0:T(8,128)(2,1)} %ham.1, f32[6,1024]{1,0:T(8,128)} %cv_in.1, f32[2,6]{1,0:T(2,128)} %coup_in.1, ...), custom_call_target="tpu_custom_call" | custom-call | tf_op jit(solution)/shard_map/section/pallas_call | solution.py:444
  54.3 1.8 %leave.1 = (f32[3,2,64,1024]{3,2,1,0:T(8,128)}, f32[3,2,64,1024]{3,2,1,0:T(8,128)}) custom-call(f32[3,2,64,1024]{3,2,1,0:T(8,128)S(1)} %get-tuple-element.4.slope, f32[3,2,64,1024]{3,2,1,0:T(8,128)S(1)} %get-tuple-element.5.acc), custom_call_target="tpu_custom_call" | custom-call | tf_op jit(solution)/shard_map/leave/pallas_call | solution.py:498
